TPU v7x, 32 devices: a whole 2x2x4 slice. The times are simulated.
32 devices in a mesh: grp: 4 (over z), pen: 8 (over y, x, core).
Axes of the slice: x: 2, y: 2, z: 4, core: 2. Of those that a mesh axis runs over, the one named last changes fastest.
Arguments:
- cell_offsets: int32 [2, 1048576], P(None, ('grp', 'pen')), may hold values from 0 to 1
- cell_z: int32 [1048576], P(('grp', 'pen')), may hold values from 0 to 255
- frac: float32 [3, 1048576], P(None, ('grp', 'pen')), may hold values from 0 to 1
- charges: float32 [1048576], P(('grp', 'pen')), may hold values from -4 to 4
- tile_counts: int32 [16384], P(('grp', 'pen')), may hold values from 16 to 64, as said below
Outputs:
- forces: float32 [3, 1048576], P(None, ('grp', 'pen'))
- energy: float32 [], replicated
Inputs may be any that keep to these rules, and one draw needn't show every extreme that they name: `tile_counts`: live slots of each tile; some tile holds 64.
All inputs are finite; a program needn't handle non-finite values.
Results may differ from a plain program's by a relative error of at most 0.0003.
Values sent between devices are 32-bit elements; how exact they have to be, the bound alone decides.
A program may use at most 256 MiB of HBM per device.

v0:
```python
import math
import jax
import jax.numpy as jnp
from jax import lax
from jax.sharding import PartitionSpec as P

KX = 256
KY = 256
KZ = 256
ATOMS = 1048576
ewald_split = 0.6
highest = lax.Precision.HIGHEST


def shifted(block, axis, distance):
    devices = range(lax.axis_size(axis))
    route = [((i - distance) % len(devices), i) for i in devices]
    return lax.ppermute(block, axis, route)


def spline_rows(fracs):
    values = [jnp.ones_like(fracs)]
    fifth = values
    for order in range(2, 7):
        nxt = []
        for j in range(order):
            term = jnp.zeros_like(fracs)
            if j >= 1:
                term = values[j - 1] * (fracs + order - 1 - j)
            if j <= order - 2:
                term = term + values[j] * (1.0 - fracs + j)
            nxt.append(term / (order - 1))
        if order == 5:
            fifth = nxt
        values = nxt
    slopes = []
    for j in range(6):
        term = jnp.zeros_like(fracs)
        if j >= 1:
            term = fifth[j - 1]
        if j <= 4:
            term = term - fifth[j]
        slopes.append(term)
    return (values, slopes)


def tile_weights(offsets, zcell, fracs, charge, counts, size_z):
    slots = charge.shape[-1]
    live = (jnp.arange(slots, dtype=jnp.int32) < counts[..., None]).astype(jnp.float32)
    live_q = charge * live
    theta_x, slope_x = spline_rows(fracs[0])
    theta_y, slope_y = spline_rows(fracs[1])
    theta_z, slope_z = spline_rows(fracs[2])
    footing = jnp.arange(8, dtype=jnp.int32)[:, None]
    cells = jnp.arange(size_z, dtype=jnp.int32)
    weight_x = 0.0
    grade_x = 0.0
    weight_y = 0.0
    grade_y = 0.0
    weight_z = 0.0
    grade_z = 0.0
    for j in range(6):
        hit_x = (footing == offsets[0][..., None, :] + j).astype(jnp.float32)
        hit_y = (footing == offsets[1][..., None, :] + j).astype(jnp.float32)
        hit_z = (cells == (zcell[..., :, None] + j) % size_z).astype(jnp.float32)
        weight_x = weight_x + theta_x[j][..., None, :] * hit_x
        grade_x = grade_x + slope_x[j][..., None, :] * hit_x
        weight_y = weight_y + theta_y[j][..., None, :] * hit_y
        grade_y = grade_y + slope_y[j][..., None, :] * hit_y
        weight_z = weight_z + theta_z[j][..., :, None] * hit_z
        grade_z = grade_z + slope_z[j][..., :, None] * hit_z
    return (weight_x, grade_x, weight_y, grade_y, weight_z, grade_z, live_q)


def modulus(index, length):
    coeffs = (1.0 / 120.0, 26.0 / 120.0, 66.0 / 120.0, 26.0 / 120.0, 1.0 / 120.0)
    real_part = 0.0
    imag_part = 0.0
    for j in range(5):
        angle = (index * j % length).astype(jnp.float32) * (2.0 * math.pi / length)
        real_part = real_part + coeffs[j] * jnp.cos(angle)
        imag_part = imag_part + coeffs[j] * jnp.sin(angle)
    return real_part * real_part + imag_part * imag_part


def influence(index_x, index_y, index_z):
    freq_x = jnp.where(2 * index_x < KX, index_x, index_x - KX).astype(jnp.float32) / KX
    freq_y = jnp.where(2 * index_y < KY, index_y, index_y - KY).astype(jnp.float32) / KY
    freq_z = jnp.where(2 * index_z < KZ, index_z, index_z - KZ).astype(jnp.float32) / KZ
    square = freq_x * freq_x + freq_y * freq_y + freq_z * freq_z
    safe = jnp.where(square > 0, square, 1.0)
    volume = float(KX * KY * KZ)
    value = jnp.exp(-math.pi**2 * safe / ewald_split**2) / (math.pi * volume * safe)
    value = value / (modulus(index_x, KX) * modulus(index_y, KY) * modulus(index_z, KZ))
    return jnp.where(square > 0, value, 0.0)


def dft_tables(length):
    index = jnp.arange(length, dtype=jnp.int32)
    angle = (index[:, None] * index[None, :] % length).astype(jnp.float32) * (
        2.0 * math.pi / length
    )
    return (jnp.cos(angle), jnp.sin(angle))


def z_slots(groups):
    planes = KZ // (2 * groups) + 1
    owner = jnp.arange(groups, dtype=jnp.int32)[:, None]
    within = jnp.arange(planes, dtype=jnp.int32)[None, :]
    ordinary = owner * (planes - 1) + within
    frequency = jnp.where(within < planes - 1, ordinary, jnp.where(owner == 0, KZ // 2, 0))
    plane_weight = jnp.where(
        within < planes - 1, jnp.where(frequency == 0, 1.0, 2.0), jnp.where(owner == 0, 1.0, 0.0)
    )
    frequency = frequency.reshape(-1)
    plane_weight = plane_weight.reshape(-1).astype(jnp.float32)
    position = jnp.arange(KZ, dtype=jnp.int32)
    angle = (frequency[:, None] * position[None, :] % KZ).astype(jnp.float32) * (2.0 * math.pi / KZ)
    usable = (plane_weight > 0).astype(jnp.float32)[:, None]
    return (planes, frequency, plane_weight, jnp.cos(angle) * usable, jnp.sin(angle) * usable)


def forward_complex(data, cos_table, sin_table, shape, axis):
    direct = jnp.dot(cos_table, data, precision=highest).reshape(shape)
    other = jnp.dot(sin_table, data, precision=highest).reshape(shape)
    real_part = jnp.take(direct, 0, axis=axis) + jnp.take(other, 1, axis=axis)
    imag_part = jnp.take(direct, 1, axis=axis) - jnp.take(other, 0, axis=axis)
    return (real_part, imag_part)


def inverse_complex(data, cos_table, sin_table, shape, axis):
    direct = jnp.dot(cos_table, data, precision=highest).reshape(shape)
    other = jnp.dot(sin_table, data, precision=highest).reshape(shape)
    real_part = jnp.take(direct, 0, axis=axis) - jnp.take(other, 1, axis=axis)
    imag_part = jnp.take(other, 0, axis=axis) + jnp.take(direct, 1, axis=axis)
    return (real_part, imag_part)


def spectrum_pen_first(grid, block_x, block_y):
    cos_x, sin_x = dft_tables(KX)
    cos_y, sin_y = dft_tables(KY)
    planes, frequency, plane_weight, cos_z, sin_z = z_slots(lax.axis_size("pen"))
    slot_total = cos_z.shape[0]
    lines = KY // lax.axis_size("grp")
    real_z = jnp.einsum("xyz,kz->ykx", grid, cos_z, precision=highest)
    imag_z = -jnp.einsum("xyz,kz->ykx", grid, sin_z, precision=highest)
    outgoing = jnp.stack([real_z, imag_z], axis=2).reshape(block_y, slot_total * 2 * block_x)
    columns = lax.all_to_all(outgoing, "pen", split_axis=1, concat_axis=0, tiled=True)
    real_y, imag_y = forward_complex(columns, cos_y, sin_y, (KY, planes, 2, block_x), 2)
    sectioned = jnp.transpose(jnp.stack([real_y, imag_y], axis=-1), (2, 0, 1, 3)).reshape(
        block_x, KY * planes * 2
    )
    rows = lax.all_to_all(sectioned, "grp", split_axis=1, concat_axis=0, tiled=True)
    real_x, imag_x = forward_complex(rows, cos_x, sin_x, (KX, lines, planes, 2), 3)
    first = lax.axis_index("pen") * planes
    index_x = jnp.arange(KX, dtype=jnp.int32)[:, None, None]
    index_y = lax.axis_index("grp") * lines + jnp.arange(lines, dtype=jnp.int32)[None, :, None]
    index_z = lax.dynamic_slice_in_dim(frequency, first, planes)[None, None, :]
    local_weight = lax.dynamic_slice_in_dim(plane_weight, first, planes)[None, None, :]
    kernel = influence(index_x, index_y, index_z)
    spectral = 0.5 * jnp.sum(local_weight * kernel * (real_x * real_x + imag_x * imag_x))
    scaled = jnp.stack([kernel * real_x, kernel * imag_x], axis=-1).reshape(KX, lines * planes * 2)
    real_b, imag_b = inverse_complex(scaled, cos_x, sin_x, (KX, lines, planes, 2), 3)
    returning = jnp.stack([real_b, imag_b], axis=-1).reshape(KX, lines * planes * 2)
    rows_home = lax.all_to_all(returning, "grp", split_axis=0, concat_axis=1, tiled=True)
    rows_home = jnp.transpose(rows_home.reshape(block_x, KY, planes, 2), (1, 2, 3, 0)).reshape(
        KY, planes * 2 * block_x
    )
    real_c, imag_c = inverse_complex(rows_home, cos_y, sin_y, (KY, planes, 2, block_x), 2)
    leaving = jnp.stack([real_c, imag_c], axis=2).reshape(KY, planes * 2 * block_x)
    home = lax.all_to_all(leaving, "pen", split_axis=0, concat_axis=1, tiled=True).reshape(
        block_y, slot_total, 2, block_x
    )
    potential = jnp.einsum(
        "ykx,kz->xyz", home[:, :, 0], plane_weight[:, None] * cos_z, precision=highest
    )
    potential = potential - jnp.einsum(
        "ykx,kz->xyz", home[:, :, 1], plane_weight[:, None] * sin_z, precision=highest
    )
    return (potential, spectral)


def place_tiles(spread, tiles_x, tiles_y):
    shaped = spread.reshape(tiles_x, tiles_y, 4, 2, 4, 2, KZ)
    total = 0.0
    for i in range(4):
        for j in range(4):
            part = jnp.transpose(shaped[:, :, i, :, j], (0, 2, 1, 3, 4)).reshape(
                2 * tiles_x, 2 * tiles_y, KZ
            )
            total = total + jnp.pad(part, ((2 * i, 6 - 2 * i), (2 * j, 6 - 2 * j), (0, 0)))
    return total


def gather_tiles(extended, tiles_x, tiles_y):
    blocks = []
    for i in range(4):
        members = []
        for j in range(4):
            part = extended[2 * i : 2 * i + 2 * tiles_x, 2 * j : 2 * j + 2 * tiles_y]
            part = part.reshape(tiles_x, 2, tiles_y, 2, KZ)
            members.append(jnp.transpose(part, (0, 2, 1, 3, 4)))
        blocks.append(jnp.stack(members, axis=3))
    return jnp.stack(blocks, axis=2).reshape(tiles_x, tiles_y, 64, KZ)


def local(cell_offsets, cell_z, frac, charges, tile_counts):
    block_x = KX // lax.axis_size("grp")
    block_y = KY // lax.axis_size("pen")
    tiles_x = block_x // 2
    tiles_y = block_y // 2
    slots = charges.shape[0] // (tiles_x * tiles_y)
    offsets = cell_offsets.reshape(2, tiles_x, tiles_y, slots)
    zcell = cell_z.reshape(tiles_x, tiles_y, slots)
    fracs = frac.reshape(3, tiles_x, tiles_y, slots)
    charge = charges.reshape(tiles_x, tiles_y, slots)
    counts = tile_counts.reshape(tiles_x, tiles_y)
    weight_x, grade_x, weight_y, grade_y, weight_z, grade_z, live_q = tile_weights(
        offsets, zcell, fracs, charge, counts, KZ
    )
    pair = weight_x[..., :, None, :] * weight_y[..., None, :, :] * live_q[..., None, None, :]
    pair = pair.reshape(tiles_x, tiles_y, 64, slots)
    spread = jnp.einsum("abfs,absz->abfz", pair, weight_z, precision=highest)
    padded = place_tiles(spread, tiles_x, tiles_y)
    rim_y = shifted(padded[: block_x + 5, block_y : block_y + 5], "pen", 1)
    merged = padded[: block_x + 5, :block_y].at[:, :5].add(rim_y)
    rim_x = shifted(merged[block_x : block_x + 5], "grp", 1)
    grid = merged[:block_x].at[:5].add(rim_x)
    potential, spectral = spectrum_pen_first(grid, block_x, block_y)
    upper = shifted(potential[:5], "grp", -1)
    ext_x = jnp.concatenate([potential, upper, jnp.zeros((1, block_y, KZ), jnp.float32)], axis=0)
    beside = shifted(ext_x[:, :5], "pen", -1)
    extended = jnp.concatenate(
        [ext_x, beside, jnp.zeros((block_x + 6, 1, KZ), jnp.float32)], axis=1
    )
    footing = gather_tiles(extended, tiles_x, tiles_y)
    main = jnp.einsum("abfz,absz->abfs", footing, weight_z, precision=highest).reshape(
        tiles_x, tiles_y, 8, 8, slots
    )
    tilt = jnp.einsum("abfz,absz->abfs", footing, grade_z, precision=highest).reshape(
        tiles_x, tiles_y, 8, 8, slots
    )
    force_x = -live_q * jnp.einsum(
        "abxs,abys,abxys->abs", grade_x, weight_y, main, precision=highest
    )
    force_y = -live_q * jnp.einsum(
        "abxs,abys,abxys->abs", weight_x, grade_y, main, precision=highest
    )
    force_z = -live_q * jnp.einsum(
        "abxs,abys,abxys->abs", weight_x, weight_y, tilt, precision=highest
    )
    total = lax.psum(spectral, ("grp", "pen"))
    forces = jnp.stack([force_x, force_y, force_z], axis=0).reshape(3, tiles_x * tiles_y * slots)
    return (forces, total / ATOMS)


def solution(mesh):
    in_specs = (
        P(None, ("grp", "pen")),
        P(("grp", "pen")),
        P(None, ("grp", "pen")),
        P(("grp", "pen")),
        P(("grp", "pen")),
    )
    out_specs = (P(None, ("grp", "pen")), P())
    return jax.shard_map(local, mesh=mesh, in_specs=in_specs, out_specs=out_specs, check_vma=False)
```

profile of v0, /device:TPU:0, one launch (start us, length us, event | category | flops | bytes accessed | tf_op | source)
XLA Modules:
  0.0 1138.8 jit_solution(11327651914012425456)
XLA Ops:
  22.6 140.7 %fusion.15 = f32[32,16,64,256]{3,2,1,0:T(8,128)} fusion(f32[32,16,64]{2,1,0:T(8,128)S(1)} %copy-done.60, s32[32,16,64]{2,1,0:T(8,128)S(1)} %get-tuple-element.184, f32[32,16,64]{2,1,0:T(8,128)S(1)} %copy-done.58, s32[32,16,64]{2,1,0:T(8,128)S(1)} %get-tuple-element.183, f32[32,16,64]{2,1,0:T(8,128)S(1)} %copy-done.54, ...), kind=kOutput, calls=%fused_computation.27 | convolution fusion | flops 6589251584 | bytes 37355520 | tf_op jit(solution)/shard_map/abfs,absz->abfz/dot_general | solution.py:223
  163.2 39.0 %reshape.1907 = f32[32,16,4,2,4,2,256]{6,5,4,3,2,1,0:T(2,128)} reshape(f32[32,16,64,256]{3,2,1,0:T(8,128)} %fusion.15) | data formatting | bytes 67108864 | tf_op jit(solution)/shard_map/reshape | solution.py:184
  202.2 25.3 %slice_bitcast_fusion.15 = (f32[32,2,16,2,256]{4,3,1,2,0:T(2,128)S(1)}, f32[32,2,16,2,256]{4,3,1,2,0:T(2,128)S(1)}, f32[32,2,16,2,256]{4,3,1,2,0:T(2,128)}, f32[...) fusion(f32[32,16,4,2,4,2,256]{6,5,4,3,2,1,0:T(2,128)} %reshape.1907), kind=kLoop, calls=%fused_computation.93 | loop fusion | bytes 67108864 | tf_op jit(solution)/shard_map/transpose | solution.py:188
  348.2 12.9 %pad_add_fusion = f32[70,38,256]{2,0,1:T(8,128)S(1)} fusion(f32[64,32,256]{2,0,1:T(8,128)} %reshape.1923, f32[64,32,256]{2,0,1:T(8,128)} %reshape.1922, f32[64,32,256]{2,0,1:T(8,128)} %reshape.1921, f32[64,32,256]{2,0,1:T(8,128)} %reshape.1920, f32[64,32,256]{2,0,1:T(8,128)} %reshape.1919, f32[64,32,256]{2,0,1:T(8,128)} %reshape.1918, ...), kind=kLoop, calls=%fused_computation.52 | loop fusion | flops 10214400 | bytes 36278272 | tf_op jit(solution)/shard_map/add | solution.py:191
  389.0 7.5 copy.290
  401.6 31.4 %all_to_all.70 = f32[32,8,2176]{2,0,1:T(8,128)} all-to-all(f32[32,8,2176]{2,0,1:T(8,128)S(1)} %copy.291), channel_id=1, replica_groups=mesh['grp'=4,'pen'=8] {'pen'}, dimensions={1} | all-to-all | bytes 4456448 | tf_op jit(solution)/shard_map/all_to_all | solution.py:148
  456.4 50.4 %all-to-all-done.1 = f32[64,4,2176]{2,0,1:T(8,128)S(1)} async-done(((f32[64,4,2176]{2,0,1:T(8,128)}), f32[64,4,2176]{2,0,1:T(8,128)S(1)}, u32[]{:S(2)}, u32[]{:S(2)}) %all-to-all-start.1) | async-done | bytes 2228256 | tf_op jit(solution)/shard_map/all_to_all | solution.py:153
  544.6 54.0 %all_to_all.71 = f32[4,64,2176]{2,1,0:T(8,128)} all-to-all(f32[4,64,2176]{2,1,0:T(8,128)S(1)} %copy.311), channel_id=1, replica_groups=mesh['grp'=4,'pen'=8] {'grp'}, dimensions={0} | all-to-all | bytes 4456448 | tf_op jit(solution)/shard_map/all_to_all | solution.py:165
  603.4 7.0 copy.372
  610.4 6.1 copy.313
  634.5 30.8 %all_to_all.72 = f32[8,32,2176]{2,1,0:T(8,128)S(1)} all-to-all(f32[8,32,2176]{2,1,0:T(8,128)S(1)} %all_to_all.63), channel_id=1, replica_groups=mesh['grp'=4,'pen'=8] {'pen'}, dimensions={0} | all-to-all | bytes 4456448 | tf_op jit(solution)/shard_map/all_to_all | solution.py:171
  670.7 8.8 fusion.280
  679.5 5.8 copy.378
  685.4 5.3 fusion.141
  701.5 55.4 %select_add_fusion.1.clone.4 = f32[32,16,64,256]{3,2,1,0:T(8,128)} fusion(f32[32,16,64]{2,1,0:T(8,128)S(1)} %copy-done.61, s32[32,16,64]{2,1,0:T(8,128)S(1)} %copy-done.43, f32[32,16,64]{2,1,0:T(8,128)S(1)} %copy-done.59, s32[32,16,64]{2,1,0:T(8,128)S(1)} %copy-done.41, f32[32,16,64]{2,1,0:T(8,128)S(1)} %copy-done.55, ...), kind=kLoop, calls=%fused_computation.13.clone.clone.clone.clone.1 | loop fusion | flops 142606336 | bytes 35127296 | tf_op jit(solution)/shard_map/abxs,abys,abxys->abs/dot_general | solution.py:243
  758.3 55.3 %fusion.294 = f32[32,16,64,256]{3,2,1,0:T(8,128)} fusion(f32[32,16,64]{2,1,0:T(8,128)S(1)} %copy-done.53, f32[32,16,64]{2,1,0:T(8,128)S(1)} %copy-done.51, f32[32,16,64]{2,1,0:T(8,128)S(1)} %copy-done.50, f32[32,16,64]{2,1,0:T(8,128)S(1)} %copy-done.52, f32[32,16,64]{2,1,0:T(8,128)S(1)} %copy-done.49, f32[32,16,64]{2,1,0:T(8,128)S(1)} %copy-done.48, ...), kind=kLoop, calls=%fused_computation.2.clone.clone.clone.1 | loop fusion | flops 142606336 | bytes 35127296 | tf_op jit(solution)/shard_map/abfz,absz->abfs/dot_general | solution.py:240
  814.3 38.4 %psum.7 = f32[]{:T(128)} all-reduce(f32[]{:T(128)S(6)} %mul_shard_map.3), channel_id=1, replica_groups=mesh['grp'=4,'pen'=8] {'grp','pen'}, use_global_device_ids=true, to_apply=%region_1.6 | all-reduce | flops 1 | bytes 8 | tf_op jit(solution)/shard_map/psum | solution.py:252
  869.1 6.2 fusion.282
  916.1 6.8 maximum_bitcast_fusion
  939.1 18.5 %pad_maximum_fusion = f32[32,16,4,2,4,2,256]{6,3,0,5,1,4,2:T(2,128)} fusion(f32[32,16,1,2,4,2,256]{6,3,0,5,1,4,2:T(2,128)} %maximum_bitcast_fusion.3, f32[32,16,1,2,4,2,256]{6,3,0,5,1,4,2:T(2,128)} %maximum_bitcast_fusion.2, f32[32,16,1,2,4,2,256]{6,3,0,5,1,4,2:T(2,128)S(1)} %maximum_bitcast_fusion.1, f32[32,16,1,2,4,2,256]{6,3,0,5,1,4,2:T(2,128)S(1)} %maximum_bitcast_fusion), kind=kLoop, calls=%fused_computation | loop fusion | flops 25165824 | bytes 67108864 | tf_op jit(solution)/shard_map/stack | solution.py:204
  957.5 46.1 %copy.321 = f32[32,16,4,2,4,2,256]{6,5,4,3,2,1,0:T(2,128)} copy(f32[32,16,4,2,4,2,256]{6,3,0,5,1,4,2:T(2,128)} %pad_maximum_fusion) | data formatting | bytes 67108864 | tf_op jit(solution)/shard_map/stack | solution.py:204
  1003.6 39.9 %reshape.1944 = f32[32,16,64,256]{3,2,1,0:T(8,128)} reshape(f32[32,16,4,2,4,2,256]{6,5,4,3,2,1,0:T(2,128)} %copy.321) | data formatting | bytes 67108864 | tf_op jit(solution)/shard_map/reshape | solution.py:204
  1043.6 42.5 %fusion.12 = f32[32,16,64,8]{2,3,1,0:T(8,128)} fusion(f32[32,16,64,8]{2,3,1,0:T(8,128)S(1)} %bitcast.442, f32[32,16,64,256]{3,2,1,0:T(8,128)} %reshape.1944, f32[32,16,64,256]{3,2,1,0:T(8,128)} %fusion.294), kind=kOutput, calls=%fused_computation.21 | convolution fusion | flops 6446383104 | bytes 69206016 | tf_op jit(solution)/shard_map/abfz,absz->abfs/dot_general | solution.py:240
  1086.1 41.7 %fusion.13 = (f32[32,16,64,8]{2,3,1,0:T(8,128)}, f32[32,16,64,8]{2,3,1,0:T(8,128)}) fusion(f32[32,16,64,8]{2,3,1,0:T(8,128)} %get-tuple-element.128, f32[32,16,64,8]{2,3,1,0:T(8,128)S(1)} %bitcast.443, f32[32,16,64,256]{3,2,1,0:T(8,128)} %reshape.1944, f32[32,16,64,256]{3,2,1,0:T(8,128)} %select_add_fusion.1.clone.4), kind=kOutput, calls=%fused_computation.24 | convolution fusion | flops 6450315264 | bytes 71303168 | tf_op jit(solution)/shard_map/abfz,absz->abfs/dot_general | solution.py:237
  (351 shorter events, 358.0 us)
Async XLA Ops:
  13.3 7.9 copy-start.32
  13.3 7.9 copy-start.34
  13.3 7.8 copy-start.36
  13.3 7.8 copy-start.38
  13.4 7.8 copy-start.40
  13.4 7.8 copy-start.42
  361.1 8.6 collective-permute-start
  371.5 9.1 collective-permute-start.1
  451.8 55.0 %all-to-all-start.1 = ((f32[64,4,2176]{2,0,1:T(8,128)}), f32[64,4,2176]{2,0,1:T(8,128)S(1)}, u32[]{:S(2)}, u32[]{:S(2)}) async-start(f32[64,4,2176]{2,0,1:T(8,128)} %copy.297), calls=%async_computation.1 | async-start | bytes 4456448 | tf_op jit(solution)/shard_map/all_to_all | solution.py:153
  699.9 57.0 %collective-permute-start.2 = (f32[5,32,256]{2,0,1:T(8,128)S(1)}, f32[5,32,256]{2,0,1:T(8,128)S(1)}, u32[]{:S(2)}, u32[]{:S(2)}) collective-permute-start(f32[5,32,256]{2,0,1:T(8,128)S(1)} %slice.369), channel_id=1, source_target_pairs={{8,0},{16,8},{24,16},{0,24},{9,1},{17,9},{25,17},{1,25},{10,2},{18... | collective-permute-start | bytes 491528 | tf_op jit(solution)/shard_map/ppermute | solution.py:18
  757.0 111.8 %collective-permute-start.3 = (f32[70,5,256]{2,0,1:T(8,128)S(1)}, f32[70,5,256]{2,0,1:T(8,128)S(1)}, u32[]{:S(2)}, u32[]{:S(2)}) collective-permute-start(f32[70,5,256]{2,0,1:T(8,128)S(1)} %pad_maximum_fusion.10), channel_id=1, source_target_pairs={{1,0},{2,1},{3,2},{4,3},{5,4},{6,5},{7,6},{0,7},{9,8},{10,9},{11,1... | collective-permute-start | bytes 1075208 | tf_op jit(solution)/shard_map/ppermute | solution.py:18
  916.0 6.8 copy-start.10
  916.0 6.8 copy-start.11
  916.1 6.8 copy-start.12
  916.1 6.8 copy-start.14
  927.4 5.3 copy-start.7
  927.5 5.6 copy-start.18
  927.5 6.4 copy-start.19
  1003.6 39.9 %copy-start.1 = (f32[32,16,8,64]{3,2,1,0:T(8,128)S(1)}, f32[32,16,8,64]{3,2,1,0:T(8,128)}, u32[]{:S(2)}) copy-start(f32[32,16,8,64]{3,2,1,0:T(8,128)} %copy-done) | copy-start | bytes 3145732
  1086.1 41.7 %copy-start.21 = (s32[32,16,64]{2,1,0:T(8,128)S(1)}, s32[32,16,64]{2,1,0:T(8,128)}, u32[]{:S(2)}) copy-start(s32[32,16,64]{2,1,0:T(8,128)} %copy-done.20) | copy-start | bytes 393220
  1086.1 41.7 %copy-start.23 = (s32[32,16,64]{2,1,0:T(8,128)S(1)}, s32[32,16,64]{2,1,0:T(8,128)}, u32[]{:S(2)}) copy-start(s32[32,16,64]{2,1,0:T(8,128)} %copy-done.22) | copy-start | bytes 393220
  1086.1 41.7 %copy-start.25 = (s32[32,16,64]{2,1,0:T(8,128)S(1)}, s32[32,16,64]{2,1,0:T(8,128)}, u32[]{:S(2)}) copy-start(s32[32,16,64]{2,1,0:T(8,128)} %copy-done.24) | copy-start | bytes 393220
  1086.1 41.7 %copy-start.27 = (s32[32,16,64]{2,1,0:T(8,128)S(1)}, s32[32,16,64]{2,1,0:T(8,128)}, u32[]{:S(2)}) copy-start(s32[32,16,64]{2,1,0:T(8,128)} %copy-done.26) | copy-start | bytes 393220
  1086.1 41.7 %copy-start.29 = (s32[32,16,64]{2,1,0:T(8,128)S(1)}, s32[32,16,64]{2,1,0:T(8,128)}, u32[]{:S(2)}) copy-start(s32[32,16,64]{2,1,0:T(8,128)} %copy-done.28) | copy-start | bytes 393220
  (76 other events, 256.3 us)
where the time goes:
time: 1150 us; the launch traced here: 1140 us
  local copies, waits for them, and re-layouts  445 us (39%)
  matrix products  265 us (23%)
  other arithmetic  200 us (17%)
  blocking collectives  155 us (13%)
  waiting for transfers between devices  60.1 us (5%)
    dot_general x1, matrix products, local(): spread = jnp.einsum('abfs,absz->abfz', pair, weight_z, precision=highest)  141 us
    transpose x17, local copies, waits for them, and re-layouts, place_tiles(): jnp.transpose(shaped[:, :, i, :, j], (0, 2, 1, 3, 4))  86.3 us
    dot_general x2, other arithmetic, local(): jnp.einsum('abxs,abys,abxys->abs', grade_x, weight_y, main, precision=hig...  60.3 us
    reshape x16, local copies, waits for them, and re-layouts, place_tiles(): jnp.transpose(shaped[:, :, i, :, j], (0, 2, 1, 3, 4))  59.5 us
    dot_general x1, other arithmetic, local(): jnp.einsum('abfz,absz->abfs', footing, grade_z, precision=highest)  55.3 us
    all_to_all x1, blocking collectives, spectrum_pen_first(): lax.all_to_all(returning, 'grp', split_axis=0, concat_axis=1, tiled=True)  54 us
    all_to_all x1, waiting for transfers between devices, spectrum_pen_first(): lax.all_to_all(sectioned, 'grp', split_axis=1, concat_axis=0, tiled=True)  50.4 us
    reshape x16, local copies, waits for them, and re-layouts, gather_tiles(): part = part.reshape(tiles_x, 2, tiles_y, 2, KZ)  50 us
  transfers between devices with their start and end apart: 5, of which 3 were waited for; matrix products, arithmetic and copies ran while one was open for 12% of the time, Pallas kernels for 0%

commit v1 on v0

--- a/solution.py
+++ b/solution.py
@@ -10,6 +10,18 @@
 ATOMS = 1048576
 ewald_split = 0.6
 highest = lax.Precision.HIGHEST
+
+
+def cut_along(shard, dim, size):
+    shape = shard.shape
+    parts = shard.reshape(*shape[:dim], size, shape[dim] // size, *shape[dim + 1 :])
+    return jnp.moveaxis(parts, dim, 0)
+
+
+def laid_out(blocks, dim):
+    blocks = jnp.moveaxis(blocks, 0, dim)
+    dims = blocks.shape
+    return blocks.reshape(*dims[:dim], dims[dim] * dims[dim + 1], *dims[dim + 2 :])
 
 
 def shifted(block, axis, distance):
@@ -162,7 +174,17 @@
     scaled = jnp.stack([kernel * real_x, kernel * imag_x], axis=-1).reshape(KX, lines * planes * 2)
     real_b, imag_b = inverse_complex(scaled, cos_x, sin_x, (KX, lines, planes, 2), 3)
     returning = jnp.stack([real_b, imag_b], axis=-1).reshape(KX, lines * planes * 2)
-    rows_home = lax.all_to_all(returning, "grp", split_axis=0, concat_axis=1, tiled=True)
+    length_2, mine = (lax.axis_size("grp"), lax.axis_index("grp"))
+    blocks_2 = cut_along(returning, 0, length_2)
+    out = blocks_2
+    for step in range(1, length_2):
+        target, source = ((mine + step) % length_2, (mine - step) % length_2)
+        sent = lax.dynamic_index_in_dim(blocks_2, target, 0)
+        theirs = lax.ppermute(
+            sent, "grp", [(i_2, (i_2 + step) % length_2) for i_2 in range(length_2)]
+        )
+        out = lax.dynamic_update_slice_in_dim(out, theirs, source, axis=0)
+    rows_home = laid_out(out, 1)
     rows_home = jnp.transpose(rows_home.reshape(block_x, KY, planes, 2), (1, 2, 3, 0)).reshape(
         KY, planes * 2 * block_x
     )

time: 1150 us -> 1240 us (1.078)
  local copies, waits for them, and re-layouts: 445 us -> 550 us
  blocking collectives: 155 us -> 121 us
    dynamic_update_slice x0 -> x3, local copies, waits for them, and re-layouts: none -> 89.5 us  [spectrum_pen_first(): out = lax.dynamic_update_slice_in_dim(out, theirs, source, axis=0)]
    all_to_all x1 -> x0, blocking collectives: 54 us -> none  [spectrum_pen_first(): lax.all_to_all(returning, 'grp', split_axis=0, concat_axis=1, tiled=True)]
    psum x1, blocking collectives: 38.4 us -> 58.6 us  [local(): total = lax.psum(spectral, ('grp', 'pen'))]
    all_to_all x3 -> x0, local copies, waits for them, and re-layouts: 14.1 us -> none  [spectrum_pen_first(): lax.all_to_all(returning, 'grp', split_axis=0, concat_axis=1, tiled=True)]
    dynamic_slice x0 -> x4, local copies, waits for them, and re-layouts: none -> 13 us  [spectrum_pen_first(): sent = lax.dynamic_index_in_dim(blocks_2, target, 0)]
  transfers between devices with their start and end apart: 5 -> 8, of which waited for: 3 -> 4; matrix products, arithmetic and copies ran while one was open for 12% -> 16% of each run, Pallas kernels for 0% -> 0%
where the time goes in v1:
time: 1240 us; the launch traced here: 1220 us
  local copies, waits for them, and re-layouts  550 us (44%)
  matrix products  265 us (21%)
  other arithmetic  201 us (16%)
  blocking collectives  121 us (10%)
  waiting for transfers between devices  71.1 us (6%)
    dot_general x1, matrix products, local(): spread = jnp.einsum('abfs,absz->abfz', pair, weight_z, precision=highest)  141 us
    dynamic_update_slice x3, local copies, waits for them, and re-layouts, spectrum_pen_first(): out = lax.dynamic_update_slice_in_dim(out, theirs, source, axis=0)  89.5 us
    transpose x17, local copies, waits for them, and re-layouts, place_tiles(): jnp.transpose(shaped[:, :, i, :, j], (0, 2, 1, 3, 4))  86.4 us
    dot_general x2, other arithmetic, local(): jnp.einsum('abxs,abys,abxys->abs', grade_x, weight_y, main, precision=hig...  60.1 us
    reshape x16, local copies, waits for them, and re-layouts, place_tiles(): jnp.transpose(shaped[:, :, i, :, j], (0, 2, 1, 3, 4))  59.6 us
    psum x1, blocking collectives, local(): total = lax.psum(spectral, ('grp', 'pen'))  58.6 us
    dot_general x1, other arithmetic, local(): jnp.einsum('abfz,absz->abfs', footing, grade_z, precision=highest)  55.3 us
    all_to_all x1, waiting for transfers between devices, spectrum_pen_first(): lax.all_to_all(sectioned, 'grp', split_axis=1, concat_axis=0, tiled=True)  50.4 us
  transfers between devices with their start and end apart: 8, of which 4 were waited for; matrix products, arithmetic and copies ran while one was open for 16% of the time, Pallas kernels for 0%

profile of v1, /device:TPU:0, one launch (start us, length us, event | category | flops | bytes accessed | tf_op | source)
XLA Modules:
  0.0 1223.8 jit_solution(4078929496152658713)
XLA Ops:
  23.0 140.7 %fusion.15 = f32[32,16,64,256]{3,2,1,0:T(8,128)} fusion(f32[32,16,64]{2,1,0:T(8,128)S(1)} %copy-done.60, s32[32,16,64]{2,1,0:T(8,128)S(1)} %get-tuple-element.187, f32[32,16,64]{2,1,0:T(8,128)S(1)} %copy-done.58, s32[32,16,64]{2,1,0:T(8,128)S(1)} %get-tuple-element.186, f32[32,16,64]{2,1,0:T(8,128)S(1)} %copy-done.54, ...), kind=kOutput, calls=%fused_computation.27 | convolution fusion | flops 6589251584 | bytes 37355520 | tf_op jit(solution)/shard_map/abfs,absz->abfz/dot_general | solution.py:245
  163.7 39.0 %reshape.1898 = f32[32,16,4,2,4,2,256]{6,5,4,3,2,1,0:T(2,128)} reshape(f32[32,16,64,256]{3,2,1,0:T(8,128)} %fusion.15) | data formatting | bytes 67108864 | tf_op jit(solution)/shard_map/reshape | solution.py:206
  202.7 25.2 %slice_bitcast_fusion.15 = (f32[32,2,16,2,256]{4,3,1,2,0:T(2,128)S(1)}, f32[32,2,16,2,256]{4,3,1,2,0:T(2,128)S(1)}, f32[32,2,16,2,256]{4,3,1,2,0:T(2,128)}, f32[...) fusion(f32[32,16,4,2,4,2,256]{6,5,4,3,2,1,0:T(2,128)} %reshape.1898), kind=kLoop, calls=%fused_computation.93 | loop fusion | bytes 67108864 | tf_op jit(solution)/shard_map/transpose | solution.py:210
  348.8 12.9 %pad_add_fusion = f32[70,38,256]{2,0,1:T(8,128)S(1)} fusion(f32[64,32,256]{2,0,1:T(8,128)} %reshape.1914, f32[64,32,256]{2,0,1:T(8,128)} %reshape.1913, f32[64,32,256]{2,0,1:T(8,128)} %reshape.1912, f32[64,32,256]{2,0,1:T(8,128)} %reshape.1911, f32[64,32,256]{2,0,1:T(8,128)} %reshape.1910, f32[64,32,256]{2,0,1:T(8,128)} %reshape.1909, ...), kind=kLoop, calls=%fused_computation.52 | loop fusion | flops 10214400 | bytes 36278272 | tf_op jit(solution)/shard_map/add | solution.py:213
  389.7 7.5 copy.305
  402.3 31.3 %all_to_all.54 = f32[32,8,2176]{2,0,1:T(8,128)} all-to-all(f32[32,8,2176]{2,0,1:T(8,128)S(1)} %copy.306), channel_id=1, replica_groups=mesh['grp'=4,'pen'=8] {'pen'}, dimensions={1} | all-to-all | bytes 4456448 | tf_op jit(solution)/shard_map/all_to_all | solution.py:160
  456.9 50.4 %all-to-all-done.1 = f32[64,4,2176]{2,0,1:T(8,128)S(1)} async-done(((f32[64,4,2176]{2,0,1:T(8,128)}), f32[64,4,2176]{2,0,1:T(8,128)S(1)}, u32[]{:S(2)}, u32[]{:S(2)}) %all-to-all-start.1) | async-done | bytes 2228256 | tf_op jit(solution)/shard_map/all_to_all | solution.py:165
  540.8 8.2 constant_dynamic-slice_fusion.2
  557.8 11.1 collective-permute-done.2
  571.9 29.8 %dynamic_update_slice.9 = f32[4,64,2176]{1,0,2:T(4,128)} dynamic-update-slice(f32[4,64,2176]{1,0,2:T(4,128)} %reshape_reshape.6, f32[1,64,2176]{1,0,2:T(1,128)S(1)} %copy.327, s32[]{:T(128)S(6)} %select_n.427, s32[]{:T(128)} %constant.649.clone.1, s32[]{:T(128)} %constant.649.clone.1) | dynamic-update-slice | bytes 1114116 | tf_op jit(solution)/shard_map/dynamic_update_slice | solution.py:186
  603.1 29.8 %dynamic_update_slice.10 = f32[4,64,2176]{1,0,2:T(4,128)} dynamic-update-slice(f32[4,64,2176]{1,0,2:T(4,128)} %dynamic_update_slice.9, f32[1,64,2176]{1,0,2:T(1,128)S(1)} %copy.329, s32[]{:T(128)S(6)} %select_n.431, s32[]{:T(128)} %constant.649.clone.1, s32[]{:T(128)} %constant.649.clone.1) | dynamic-update-slice | bytes 1114116 | tf_op jit(solution)/shard_map/dynamic_update_slice | solution.py:186
  634.4 29.8 %dynamic_update_slice.11 = f32[4,64,2176]{1,0,2:T(4,128)} dynamic-update-slice(f32[4,64,2176]{1,0,2:T(4,128)} %dynamic_update_slice.10, f32[1,64,2176]{1,0,2:T(1,128)S(1)} %copy.331, s32[]{:T(128)S(6)} %select_n.435, s32[]{:T(128)} %constant.649.clone.1, s32[]{:T(128)} %constant.649.clone.1) | dynamic-update-slice | bytes 1114116 | tf_op jit(solution)/shard_map/dynamic_update_slice | solution.py:186
  668.9 7.1 copy.392
  700.0 30.8 %all_to_all.55 = f32[8,32,2176]{2,1,0:T(8,128)S(1)} all-to-all(f32[8,32,2176]{2,1,0:T(8,128)S(1)} %all_to_all.48), channel_id=1, replica_groups=mesh['grp'=4,'pen'=8] {'pen'}, dimensions={0} | all-to-all | bytes 4456448 | tf_op jit(solution)/shard_map/all_to_all | solution.py:193
  736.2 8.8 fusion.280
  766.5 55.3 %select_add_fusion.1.clone.4 = f32[32,16,64,256]{3,2,1,0:T(8,128)} fusion(f32[32,16,64]{2,1,0:T(8,128)S(1)} %copy-done.61, s32[32,16,64]{2,1,0:T(8,128)S(1)} %copy-done.43, f32[32,16,64]{2,1,0:T(8,128)S(1)} %copy-done.59, s32[32,16,64]{2,1,0:T(8,128)S(1)} %copy-done.41, f32[32,16,64]{2,1,0:T(8,128)S(1)} %copy-done.55, ...), kind=kLoop, calls=%fused_computation.13.clone.clone.clone.clone.1 | loop fusion | flops 142606336 | bytes 35127296 | tf_op jit(solution)/shard_map/abxs,abys,abxys->abs/dot_general | solution.py:265
  823.1 55.3 %fusion.294 = f32[32,16,64,256]{3,2,1,0:T(8,128)} fusion(f32[32,16,64]{2,1,0:T(8,128)S(1)} %copy-done.53, f32[32,16,64]{2,1,0:T(8,128)S(1)} %copy-done.51, f32[32,16,64]{2,1,0:T(8,128)S(1)} %copy-done.50, f32[32,16,64]{2,1,0:T(8,128)S(1)} %copy-done.52, f32[32,16,64]{2,1,0:T(8,128)S(1)} %copy-done.49, f32[32,16,64]{2,1,0:T(8,128)S(1)} %copy-done.48, ...), kind=kLoop, calls=%fused_computation.2.clone.clone.clone.1 | loop fusion | flops 142606336 | bytes 35127296 | tf_op jit(solution)/shard_map/abfz,absz->abfs/dot_general | solution.py:262
  879.2 58.6 %psum.7 = f32[]{:T(128)} all-reduce(f32[]{:T(128)S(6)} %mul_shard_map.3), channel_id=1, replica_groups=mesh['grp'=4,'pen'=8] {'grp','pen'}, use_global_device_ids=true, to_apply=%region_1.6 | all-reduce | flops 1 | bytes 8 | tf_op jit(solution)/shard_map/psum | solution.py:274
  1001.1 6.8 maximum_bitcast_fusion
  1024.1 18.5 %pad_maximum_fusion = f32[32,16,4,2,4,2,256]{6,3,0,5,1,4,2:T(2,128)} fusion(f32[32,16,1,2,4,2,256]{6,3,0,5,1,4,2:T(2,128)} %maximum_bitcast_fusion.3, f32[32,16,1,2,4,2,256]{6,3,0,5,1,4,2:T(2,128)} %maximum_bitcast_fusion.2, f32[32,16,1,2,4,2,256]{6,3,0,5,1,4,2:T(2,128)S(1)} %maximum_bitcast_fusion.1, f32[32,16,1,2,4,2,256]{6,3,0,5,1,4,2:T(2,128)S(1)} %maximum_bitcast_fusion), kind=kLoop, calls=%fused_computation | loop fusion | flops 25165824 | bytes 67108864 | tf_op jit(solution)/shard_map/stack | solution.py:226
  1042.6 46.1 %copy.341 = f32[32,16,4,2,4,2,256]{6,5,4,3,2,1,0:T(2,128)} copy(f32[32,16,4,2,4,2,256]{6,3,0,5,1,4,2:T(2,128)} %pad_maximum_fusion) | data formatting | bytes 67108864 | tf_op jit(solution)/shard_map/stack | solution.py:226
  1088.7 39.9 %reshape.1934 = f32[32,16,64,256]{3,2,1,0:T(8,128)} reshape(f32[32,16,4,2,4,2,256]{6,5,4,3,2,1,0:T(2,128)} %copy.341) | data formatting | bytes 67108864 | tf_op jit(solution)/shard_map/reshape | solution.py:226
  1128.7 42.5 %fusion.12 = f32[32,16,64,8]{2,3,1,0:T(8,128)} fusion(f32[32,16,64,8]{2,3,1,0:T(8,128)S(1)} %bitcast.443, f32[32,16,64,256]{3,2,1,0:T(8,128)} %reshape.1934, f32[32,16,64,256]{3,2,1,0:T(8,128)} %fusion.294), kind=kOutput, calls=%fused_computation.21 | convolution fusion | flops 6446383104 | bytes 69206016 | tf_op jit(solution)/shard_map/abfz,absz->abfs/dot_general | solution.py:262
  1171.1 41.7 %fusion.13 = (f32[32,16,64,8]{2,3,1,0:T(8,128)}, f32[32,16,64,8]{2,3,1,0:T(8,128)}) fusion(f32[32,16,64,8]{2,3,1,0:T(8,128)} %get-tuple-element.131, f32[32,16,64,8]{2,3,1,0:T(8,128)S(1)} %bitcast.444, f32[32,16,64,256]{3,2,1,0:T(8,128)} %reshape.1934, f32[32,16,64,256]{3,2,1,0:T(8,128)} %select_add_fusion.1.clone.4), kind=kOutput, calls=%fused_computation.24 | convolution fusion | flops 6450315264 | bytes 71303168 | tf_op jit(solution)/shard_map/abfz,absz->abfs/dot_general | solution.py:259
  (365 shorter events, 391.8 us)
Async XLA Ops:
  13.4 8.2 copy-start.32
  13.4 8.2 copy-start.34
  13.4 8.2 copy-start.36
  13.4 8.2 copy-start.38
  13.4 8.2 copy-start.40
  13.4 8.2 copy-start.42
  361.7 8.6 collective-permute-start
  372.1 9.2 collective-permute-start.1
  452.5 54.8 %all-to-all-start.1 = ((f32[64,4,2176]{2,0,1:T(8,128)}), f32[64,4,2176]{2,0,1:T(8,128)S(1)}, u32[]{:S(2)}, u32[]{:S(2)}) async-start(f32[64,4,2176]{2,0,1:T(8,128)} %copy.312), calls=%async_computation.1 | async-start | bytes 4456448 | tf_op jit(solution)/shard_map/all_to_all | solution.py:165
  551.2 17.7 %collective-permute-start.2 = (f32[1,64,2176]{2,1,0:T(8,128)}, f32[1,64,2176]{2,1,0:T(8,128)}, u32[]{:S(2)}, u32[]{:S(2)}) collective-permute-start(f32[1,64,2176]{2,1,0:T(8,128)} %copy.326), channel_id=1, source_target_pairs={{0,8},{8,16},{16,24},{24,0},{1,9},{9,17},{17,25},{25,1},{2,10},{10... | collective-permute-start | bytes 1671176 | tf_op jit(solution)/shard_map/ppermute | solution.py:183
  552.5 49.2 %collective-permute-start.3 = (f32[1,64,2176]{2,1,0:T(8,128)S(1)}, f32[1,64,2176]{2,1,0:T(8,128)S(1)}, u32[]{:S(2)}, u32[]{:S(2)}) collective-permute-start(f32[1,64,2176]{2,1,0:T(8,128)S(1)} %copy.328), channel_id=1, source_target_pairs={{0,16},{8,24},{16,0},{24,8},{1,17},{9,25},{17,1},{25,9},{2,18},{10... | collective-permute-start | bytes 1671176 | tf_op jit(solution)/shard_map/ppermute | solution.py:183
  555.9 77.1 %collective-permute-start.4 = (f32[1,64,2176]{2,1,0:T(8,128)S(1)}, f32[1,64,2176]{2,1,0:T(8,128)S(1)}, u32[]{:S(2)}, u32[]{:S(2)}) collective-permute-start(f32[1,64,2176]{2,1,0:T(8,128)S(1)} %copy.330), channel_id=1, source_target_pairs={{0,24},{8,0},{16,8},{24,16},{1,25},{9,1},{17,9},{25,17},{2,26},{10... | collective-permute-start | bytes 1671176 | tf_op jit(solution)/shard_map/ppermute | solution.py:183
  765.2 56.6 %collective-permute-start.5 = (f32[5,32,256]{2,0,1:T(8,128)S(1)}, f32[5,32,256]{2,0,1:T(8,128)S(1)}, u32[]{:S(2)}, u32[]{:S(2)}) collective-permute-start(f32[5,32,256]{2,0,1:T(8,128)S(1)} %slice.369), channel_id=1, source_target_pairs={{8,0},{16,8},{24,16},{0,24},{9,1},{17,9},{25,17},{1,25},{10,2},{18... | collective-permute-start | bytes 491528 | tf_op jit(solution)/shard_map/ppermute | solution.py:30
  821.9 132.0 %collective-permute-start.6 = (f32[70,5,256]{2,0,1:T(8,128)S(1)}, f32[70,5,256]{2,0,1:T(8,128)S(1)}, u32[]{:S(2)}, u32[]{:S(2)}) collective-permute-start(f32[70,5,256]{2,0,1:T(8,128)S(1)} %pad_maximum_fusion.10), channel_id=1, source_target_pairs={{1,0},{2,1},{3,2},{4,3},{5,4},{6,5},{7,6},{0,7},{9,8},{10,9},{11,1... | collective-permute-start | bytes 1075208 | tf_op jit(solution)/shard_map/ppermute | solution.py:30
  1001.1 6.8 copy-start.10
  1001.1 6.8 copy-start.11
  1001.1 6.8 copy-start.12
  1001.1 6.8 copy-start.14
  1088.7 39.9 %copy-start.1 = (f32[32,16,8,64]{3,2,1,0:T(8,128)S(1)}, f32[32,16,8,64]{3,2,1,0:T(8,128)}, u32[]{:S(2)}) copy-start(f32[32,16,8,64]{3,2,1,0:T(8,128)} %copy-done) | copy-start | bytes 3145732
  1171.1 41.7 %copy-start.21 = (s32[32,16,64]{2,1,0:T(8,128)S(1)}, s32[32,16,64]{2,1,0:T(8,128)}, u32[]{:S(2)}) copy-start(s32[32,16,64]{2,1,0:T(8,128)} %copy-done.20) | copy-start | bytes 393220
  1171.1 41.7 %copy-start.23 = (s32[32,16,64]{2,1,0:T(8,128)S(1)}, s32[32,16,64]{2,1,0:T(8,128)}, u32[]{:S(2)}) copy-start(s32[32,16,64]{2,1,0:T(8,128)} %copy-done.22) | copy-start | bytes 393220
  1171.1 41.7 %copy-start.25 = (s32[32,16,64]{2,1,0:T(8,128)S(1)}, s32[32,16,64]{2,1,0:T(8,128)}, u32[]{:S(2)}) copy-start(s32[32,16,64]{2,1,0:T(8,128)} %copy-done.24) | copy-start | bytes 393220
  1171.1 41.7 %copy-start.27 = (s32[32,16,64]{2,1,0:T(8,128)S(1)}, s32[32,16,64]{2,1,0:T(8,128)}, u32[]{:S(2)}) copy-start(s32[32,16,64]{2,1,0:T(8,128)} %copy-done.26) | copy-start | bytes 393220
  1171.1 41.7 %copy-start.29 = (s32[32,16,64]{2,1,0:T(8,128)S(1)}, s32[32,16,64]{2,1,0:T(8,128)}, u32[]{:S(2)}) copy-start(s32[32,16,64]{2,1,0:T(8,128)} %copy-done.28) | copy-start | bytes 393220
  (79 other events, 273.9 us)
